TPU v7x, 256 devices: a whole 4x4x8 slice. The times are simulated.
256 devices in a mesh: head: 8 (over z), tok: 32 (over x, y, core).
Axes of the slice: x: 4, y: 4, z: 8, core: 2. Of those that a mesh axis runs over, the one named last changes fastest.
Arguments:
- teacher_q: bfloat16 [4096, 2048], P('tok', 'head'), may hold values from -48 to 48
- student_q: bfloat16 [4096, 2048], P('tok', 'head'), may hold values from -48 to 48
- owner_table: int32 [32, 32], replicated, may hold values from -1 to 31, as said below
Outputs:
- student_grad: bfloat16 [4096, 2048], P('tok', 'head')
- divergence: float32 [32], P('head')
Inputs may be any that keep to these rules, and one draw needn't show every extreme that they name: `owner_table`: Symmetric; every diagonal entry is an owner; an owner is a tok index; each tok index owns at most 8 pairs i <= j, and some tok index owns exactly 8 in every draw.
All inputs are finite; a program needn't handle non-finite values.
Results may differ from a plain program's by a relative error of at most 0.0049.
Values may be sent and summed in bfloat16 or wider, within the bound.
No kernel may reach another device: no remote copies, remote signals or barrier semaphores. Data moves between devices by JAX's collectives and lax.ppermute only.
A program may use at most 64 MiB of HBM per device.

v0:
```python
import jax
import jax.numpy as jnp
from jax import lax
from jax.sharding import PartitionSpec as P

HEAD_DIM = 64


floor_value = -1e30
distill_weight = 32.0


def sent_together(arrays, axis, dim, along):
    both = jnp.concatenate(arrays, axis=along)
    whole, at, done = (lax.all_gather(both, axis, axis=dim, tiled=True), 0, [])
    for a in arrays:
        done.append(lax.slice_in_dim(whole, at, at + a.shape[along], axis=along))
        at += a.shape[along]
    return tuple(done)


def laid_out(tiles, dim):
    tiles = jnp.moveaxis(tiles, 0, dim)
    lengths = tiles.shape
    return tiles.reshape(*lengths[:dim], lengths[dim] * lengths[dim + 1], *lengths[dim + 2 :])


def copy_for_each(array, axis):
    copies = jnp.broadcast_to(array, (lax.axis_size(axis), *array.shape))
    return lax.all_to_all(copies, axis, split_axis=0, concat_axis=0, tiled=True)


def gathered_copies(array, axis, dim):
    return laid_out(copy_for_each(array, axis), dim)


def sent_together_2(arrays, axis, dim, along):
    both = jnp.concatenate(arrays, axis=along)
    whole, at, done = (gathered_copies(both, axis, dim), 0, [])
    for a in arrays:
        done.append(lax.slice_in_dim(whole, at, at + a.shape[along], axis=along))
        at += a.shape[along]
    return tuple(done)


def of_everyone(array, axis):
    return copy_for_each(array, axis).sum(axis=0)


def split_heads(block):
    return block.reshape(block.shape[0], -1, HEAD_DIM)


def tile_scores(left_block, right_block):
    return jnp.einsum(
        "ahd,bhd->hab", left_block, right_block, preferred_element_type=jnp.float32
    ) * HEAD_DIM ** (-0.5)


def reduced_totals(scores, reduce_axis):
    highest = jnp.max(scores, axis=reduce_axis)
    return (
        highest,
        jnp.sum(jnp.exp(scores - jnp.expand_dims(highest, reduce_axis)), axis=reduce_axis),
    )


def fold_totals(earlier, later):
    teacher_top = jnp.maximum(earlier[0], later[0])
    student_top = jnp.maximum(earlier[2], later[2])
    teacher_sum = earlier[1] * jnp.exp(earlier[0] - teacher_top) + later[1] * jnp.exp(
        later[0] - teacher_top
    )
    student_sum = earlier[3] * jnp.exp(earlier[2] - student_top) + later[3] * jnp.exp(
        later[2] - student_top
    )
    return (teacher_top, teacher_sum, student_top, student_sum)


def pair_totals(teacher_left, teacher_right, student_left, student_right):
    teacher_scores = tile_scores(teacher_left, teacher_right)
    student_scores = tile_scores(student_left, student_right)
    row_side = reduced_totals(teacher_scores, 2) + reduced_totals(student_scores, 2)
    column_side = reduced_totals(teacher_scores, 1) + reduced_totals(student_scores, 1)
    return (row_side, column_side)


def to_logsum(totals):
    return (totals[0] + jnp.log(totals[1]), totals[2] + jnp.log(totals[3]))


def blank_totals(head_count, block_rows):
    return (
        jnp.full((head_count, block_rows), floor_value, jnp.float32),
        jnp.zeros((head_count, block_rows), jnp.float32),
        jnp.full((head_count, block_rows), floor_value, jnp.float32),
        jnp.zeros((head_count, block_rows), jnp.float32),
    )


def gathered_block(gathered, position, block_rows):
    return split_heads(lax.dynamic_slice_in_dim(gathered, position * block_rows, block_rows, 0))


def pair_gradient(
    teacher_left, teacher_right, student_left, student_right, left_logsum, right_logsum
):
    teacher_scores = tile_scores(teacher_left, teacher_right)
    student_scores = tile_scores(student_left, student_right)
    teacher_rows = jnp.exp(teacher_scores - left_logsum[0][:, :, None])
    student_rows = jnp.exp(student_scores - left_logsum[1][:, :, None])
    teacher_cols = jnp.exp(teacher_scores - right_logsum[0][:, None, :])
    student_cols = jnp.exp(student_scores - right_logsum[1][:, None, :])
    score_gap = teacher_scores - student_scores
    symmetric = (student_rows - teacher_rows + (student_cols - teacher_cols)).astype(jnp.bfloat16)
    left_grad = jnp.einsum(
        "hab,bhd->ahd", symmetric, student_right, preferred_element_type=jnp.float32
    )
    right_grad = jnp.einsum(
        "hab,ahd->bhd", symmetric, student_left, preferred_element_type=jnp.float32
    )
    left_div = jnp.sum(teacher_rows * score_gap, axis=(1, 2))
    right_div = jnp.sum(teacher_cols * score_gap, axis=(1, 2))
    return (left_grad, right_grad, left_div, right_div)


def per_device(teacher_q, student_q, owner_table):
    block_count = lax.axis_size("tok")
    own_index = lax.axis_index("tok")
    block_rows = teacher_q.shape[0]
    row_width = teacher_q.shape[1]
    head_count = row_width // HEAD_DIM
    home_teacher = split_heads(teacher_q)
    home_student = split_heads(student_q)
    every_teacher, every_student = sent_together((teacher_q, student_q), "tok", 0, 1)
    inside_row = owner_table[own_index] >= 0
    column_total = jnp.sum(inside_row.astype(jnp.int32))
    columns = jnp.nonzero(inside_row, size=block_count, fill_value=0)[0].astype(jnp.int32)

    def row_turn(slot_index, totals):
        column = columns[slot_index]
        row_side, unused = pair_totals(
            home_teacher,
            gathered_block(every_teacher, column, block_rows),
            home_student,
            gathered_block(every_student, column, block_rows),
        )
        return fold_totals(totals, row_side)

    own_totals = lax.fori_loop(0, column_total, row_turn, blank_totals(head_count, block_rows))
    own_logsum = to_logsum(own_totals)
    every_tlog, every_slog = sent_together_2((own_logsum[0], own_logsum[1]), "tok", 1, 0)

    def gradient_turn(slot_index, carry):
        gradient, running = carry
        column = columns[slot_index]
        column_logsum = (
            lax.dynamic_slice_in_dim(every_tlog, column * block_rows, block_rows, 1),
            lax.dynamic_slice_in_dim(every_slog, column * block_rows, block_rows, 1),
        )
        pieces = pair_gradient(
            home_teacher,
            gathered_block(every_teacher, column, block_rows),
            home_student,
            gathered_block(every_student, column, block_rows),
            own_logsum,
            column_logsum,
        )
        return (gradient + pieces[0], running + pieces[2])

    start_grad = jnp.zeros((block_rows, head_count, HEAD_DIM), jnp.float32)
    gradient, divergence = lax.fori_loop(
        0, column_total, gradient_turn, (start_grad, jnp.zeros((head_count,), jnp.float32))
    )
    own_grad = gradient.reshape(block_rows, row_width)
    divergence = divergence + jnp.sum(own_logsum[1] - own_logsum[0], axis=1)
    divergence = of_everyone(divergence, "tok") / (block_rows * block_count)
    student_grad = (own_grad * (distill_weight * HEAD_DIM ** (-0.5))).astype(jnp.bfloat16)
    return (student_grad, divergence)


def solution(mesh):
    placed = (P("tok", "head"), P("tok", "head"), P())
    return jax.shard_map(
        per_device,
        mesh=mesh,
        in_specs=placed,
        out_specs=(P("tok", "head"), P("head")),
        check_vma=False,
    )
```

profile of v0, /device:TPU:32, one launch (start us, length us, event | category | flops | bytes accessed | tf_op | source)
XLA Modules:
  0.0 180.3 jit_solution(9530397728459261120)
XLA Ops:
  7.2 0.9 copy.35
  8.2 1.0 copy.36
  9.1 0.7 pad_maximum_fusion
  9.8 0.7 fusion.11
  10.8 0.8 scatter_custom_fusion
  11.8 1.3 fusion.12
  13.1 0.7 compare_select_fusion.3
  13.8 53.6 %all-gather.2.cloned.1.call-done = bf16[4096,512]{0,1:T(8,128)(2,1)} async-done(((bf16[128,512]{0,1:T(8,128)(2,1)}), bf16[4096,512]{0,1:T(8,128)(2,1)}) %all-gather.2.cloned.1.call-update) | async-done | bytes 4194320 | tf_op jit(solution)/shard_map/all_gather | solution.py:15
  67.4 3.9 %fusion.15 = (bf16[4096,256]{0,1:T(8,128)(2,1)S(1)}, bf16[4096,256]{0,1:T(8,128)(2,1)}) fusion(bf16[4096,512]{0,1:T(8,128)(2,1)} %all-gather.2.cloned.1.call-done), kind=kLoop, calls=%fused_computation.49 | loop fusion | bytes 8388608 | tf_op jit(solution)/shard_map/slice | solution.py:17
  71.3 22.2 %while.28 = (s32[]{:T(128)}, f32[4,128]{1,0:T(4,128)S(1)}, f32[4,128]{1,0:T(4,128)S(1)}, f32[4,128]{1,0:T(4,128)S(1)}, f32[4,128]{1,0:T(4,128)S(1)}, /*index=5*/...) while((s32[]{:T(128)}, f32[4,128]{1,0:T(4,128)S(1)}, ...), condition=%wide.region_9.10_spmd, body=%wide.region_4.9_spmd.sunk | while | flops 17305608 | bytes 1609977 | solution.py:150
  72.0 0.7 dynamic_slice.47
  73.4 0.3 fusion.42
  73.7 0.9 constant_dynamic-slice_fusion.10
  74.6 0.3 fusion.41
  75.6 0.7 dynamic_slice.47
  77.0 0.3 fusion.42
  77.3 0.9 constant_dynamic-slice_fusion.10
  78.1 0.3 fusion.41
  79.2 0.7 dynamic_slice.47
  80.6 0.3 fusion.42
  80.9 0.9 constant_dynamic-slice_fusion.10
  81.7 0.3 fusion.41
  82.7 0.7 dynamic_slice.47
  84.1 0.3 fusion.42
  84.5 0.9 constant_dynamic-slice_fusion.10
  86.3 0.7 dynamic_slice.47
  87.7 0.3 fusion.42
  88.0 0.9 constant_dynamic-slice_fusion.10
  89.9 0.7 dynamic_slice.47
  91.3 0.3 fusion.42
  91.6 0.9 constant_dynamic-slice_fusion.10
  93.6 0.7 broadcast_in_dim.18
  94.3 19.6 %all-to-all-start = ((f32[32,8,128]{2,1,0:T(8,128)}), f32[32,8,128]{2,1,0:T(8,128)S(1)}, u32[]{:S(2)}, u32[]{:S(2)}) async-start(f32[32,8,128]{2,1,0:T(8,128)} %broadcast_in_dim.18), calls=%async_computation | async-start | bytes 262144 | tf_op jit(solution)/shard_map/all_to_all | solution.py:30
  113.9 7.9 %all-to-all-done = f32[32,8,128]{2,1,0:T(8,128)S(1)} async-done(((f32[32,8,128]{2,1,0:T(8,128)}), f32[32,8,128]{2,1,0:T(8,128)S(1)}, u32[]{:S(2)}, u32[]{:S(2)}) %all-to-all-start) | async-done | bytes 131104 | tf_op jit(solution)/shard_map/all_to_all | solution.py:30
  121.8 24.0 %while.29 = (s32[]{:T(128)}, f32[128,4,64]{0,2,1:T(8,128)S(1)}, f32[4]{0:T(128)S(1)}, s32[]{:T(128)}, s32[32]{0:T(128)S(1)}, /*index=5*/bf16[4096,256]{0,1:T(8,1...) while((s32[]{:T(128)}, f32[128,4,64]{0,2,1:T(8,128)S(1)}, ...), condition=%wide.region_12.13_spmd, body=%wide.region_10.12_spmd.sunk | while | flops 26116104 | bytes 2181449 | solution.py:172
  122.5 0.7 dynamic_slice.50
  123.8 0.9 constant_dynamic-slice_fusion.12
  124.9 0.4 multiply_reduce_fusion.2
  125.3 0.3 fusion.48
  126.4 0.7 dynamic_slice.50
  127.7 0.9 constant_dynamic-slice_fusion.12
  128.8 0.4 multiply_reduce_fusion.2
  129.2 0.3 fusion.48
  130.2 0.7 dynamic_slice.50
  131.6 0.9 constant_dynamic-slice_fusion.12
  132.7 0.4 multiply_reduce_fusion.2
  133.1 0.3 fusion.48
  134.1 0.7 dynamic_slice.50
  135.5 0.9 constant_dynamic-slice_fusion.12
  136.6 0.4 multiply_reduce_fusion.2
  137.0 0.3 fusion.48
  138.0 0.7 dynamic_slice.50
  139.4 0.9 constant_dynamic-slice_fusion.12
  140.5 0.4 multiply_reduce_fusion.2
  140.9 0.3 fusion.48
  141.9 0.7 dynamic_slice.50
  143.3 0.9 constant_dynamic-slice_fusion.12
  144.4 0.4 multiply_reduce_fusion.2
  144.8 0.3 fusion.48
  145.8 0.6 broadcast_in_dim.23
  146.4 19.2 %all-to-all-start.1 = ((f32[32,1,4]{2,1,0:T(1,128)}), f32[32,1,4]{2,1,0:T(1,128)S(1)}, u32[]{:S(2)}, u32[]{:S(2)}) async-start(f32[32,1,4]{2,1,0:T(1,128)} %broadcast_in_dim.23), calls=%async_computation.1 | async-start | bytes 32768 | tf_op jit(solution)/shard_map/all_to_all | solution.py:30
  165.6 0.7 copy.40
  166.3 6.6 %all-to-all-done.1 = f32[32,1,4]{2,1,0:T(1,128)S(1)} async-done(((f32[32,1,4]{2,1,0:T(1,128)}), f32[32,1,4]{2,1,0:T(1,128)S(1)}, u32[]{:S(2)}, u32[]{:S(2)}) %all-to-all-start.1) | async-done | bytes 544 | tf_op jit(solution)/shard_map/all_to_all | solution.py:30
  173.0 0.5 broadcast_multiply_fusion
  (66 shorter events, 4.1 us)
Async XLA Ops:
  7.2 60.2 %all-gather.2.cloned.1.call-start = ((), (), s32[]{:S(2)}) async-start(), calls=%async_computation.2 | async-start | bytes 4325376 | tf_op jit(solution)/shard_map/all_gather | solution.py:15
  94.3 27.5 %all-to-all-start = ((f32[32,8,128]{2,1,0:T(8,128)}), f32[32,8,128]{2,1,0:T(8,128)S(1)}, u32[]{:S(2)}, u32[]{:S(2)}) async-start(f32[32,8,128]{2,1,0:T(8,128)} %broadcast_in_dim.18), calls=%async_computation | async-start | bytes 262144 | tf_op jit(solution)/shard_map/all_to_all | solution.py:30
  146.4 26.5 %all-to-all-start.1 = ((f32[32,1,4]{2,1,0:T(1,128)}), f32[32,1,4]{2,1,0:T(1,128)S(1)}, u32[]{:S(2)}, u32[]{:S(2)}) async-start(f32[32,1,4]{2,1,0:T(1,128)} %broadcast_in_dim.23), calls=%async_computation.1 | async-start | bytes 32768 | tf_op jit(solution)/shard_map/all_to_all | solution.py:30
Sparse Core Ops, SparseCore 0:
  10.5 56.8 all-gather.1
where the time goes:
time: 183 us; the launch traced here: 180 us
  waiting for transfers between devices  68 us (37%)
  starting transfers between devices  38.8 us (21%)
  local copies, waits for them, and re-layouts  26.6 us (15%)
  loops' own time  18 us (10%)
  between operations  14.1 us (8%)
  matrix products  8.65 us (5%)
  other arithmetic  6.1 us (3%)
    all_gather x1, waiting for transfers between devices, sent_together(): whole, at, done = (lax.all_gather(both, axis, axis=dim, tiled=True), 0, [])  53.6 us
    all_to_all x2, starting transfers between devices, copy_for_each(): return lax.all_to_all(copies, axis, split_axis=0, concat_axis=0, tiled=True)  38.8 us
    all_to_all x2, waiting for transfers between devices, copy_for_each(): return lax.all_to_all(copies, axis, split_axis=0, concat_axis=0, tiled=True)  14.5 us
    dynamic_slice x18, local copies, waits for them, and re-layouts, gathered_block(): lax.dynamic_slice_in_dim(gathered, position * block_rows, block_rows, 0)  10.5 us
    another operation x1, loops' own time, per_device(): lax.fori_loop(0, column_total, gradient_turn, (start_grad, jnp.zeros((hea...  9.02 us
    another operation x1, loops' own time, per_device(): lax.fori_loop(0, column_total, row_turn, blank_totals(head_count, block_r...  8.99 us
    dot_general x24, matrix products, tile_scores(): jnp.einsum('ahd,bhd->hab', left_block, right_block, preferred_element_typ...  6.57 us
    dynamic_slice x6, local copies, waits for them, and re-layouts, row_turn(): column = columns[slot_index]  4 us
  transfers between devices with their start and end apart: 3, of which 3 were waited for; matrix products, arithmetic and copies ran while one was open for 3% of the time, Pallas kernels for 0%

commit v1 on v0

v1 whole, which is shorter than its diff:
```python
import jax
import jax.numpy as jnp
from jax import lax
from jax.experimental import pallas as pl
from jax.experimental.pallas import tpu as pltpu
from jax.sharding import PartitionSpec as P

HEAD = 64
ROWS = 128
BLOCKS = 32
LINE = 4
LOG2E = 1.4426950408889634
LN2 = 0.6931471805599453
SCALE = HEAD**-0.5
WEIGHT = 32.0 * SCALE
SUM_LIMIT = 2.0**100
FLOOR = -1e30
UNROLL = 4
LIST_AT = 8
OWN_AT = LIST_AT + BLOCKS * BLOCKS + 8
PLAN_LEN = OWN_AT + LINE * BLOCKS + 8
VMEM = pl.BlockSpec(memory_space=pltpu.VMEM)
SMEM = pl.BlockSpec(memory_space=pltpu.SMEM)


def my_index():
    return lax.axis_index("tok")


def exchanged(array, bits):
    return lax.ppermute(array, "tok", [(i, i ^ bits) for i in range(BLOCKS)])


def slice_kernel(teacher_ref, student_ref, *out_refs):
    x = my_index() >> 3
    for head in range(LINE):
        at = slice(head * HEAD, head * HEAD + HEAD)
        both = jnp.concatenate([teacher_ref[:, at], student_ref[:, at]], axis=1)
        for turn, out_ref in enumerate(out_refs):

            @pl.when(x == (head ^ turn))
            def _():
                out_ref[...] = both


def plan_kernel(table_ref, plan_ref):
    me = my_index()

    def listed(row, first, prefix):
        at = first
        for column in range(BLOCKS):
            plan_ref[at] = prefix + column
            at = at + (table_ref[row, column] >= 0).astype(jnp.int32)
        return at

    end = lax.fori_loop(0, BLOCKS, lambda i, at: listed(i, at, i * BLOCKS), jnp.int32(LIST_AT))
    for k in range(UNROLL):
        plan_ref[end + k] = BLOCKS * BLOCKS
    plan_ref[0] = end - LIST_AT
    end = lax.fori_loop(
        0, LINE, lambda b, at: listed(me ^ (b << 3), at, b * BLOCKS), jnp.int32(OWN_AT)
    )
    for k in range(UNROLL):
        plan_ref[end + k] = LINE * BLOCKS
    plan_ref[1] = end - OWN_AT


def main_kernel(
    plan_ref,
    half_ref,
    other_ref,
    *refs,
):
    out_refs = refs[:LINE]
    rows_ref, wide_ref, acc_ref, top_ref, inv_ref, grad_ref, col_ref = refs[LINE:]
    me = my_index()

    for slot in range(BLOCKS):
        code = ((slot & 3) << 3) | (((slot >> 2) & 3) << 1) | (slot >> 4)
        block = me ^ code
        tile = half_ref[slot] if slot < 16 else other_ref[slot - 16]
        rows_ref[block] = tile
        flipped = tile.astype(jnp.float32).T.astype(jnp.bfloat16)
        zero = jnp.zeros((HEAD, ROWS), jnp.bfloat16)
        wide_ref[block, :, :ROWS] = jnp.concatenate([flipped[:HEAD], zero], axis=0)
        wide_ref[block, :, ROWS:] = jnp.concatenate([zero, flipped[HEAD:]], axis=0)
    wide_ref[BLOCKS] = jnp.zeros((ROWS, 2 * ROWS), jnp.bfloat16)
    pairs = plan_ref[0]
    own_pairs = plan_ref[1]

    def scores(left, right):
        return jnp.dot(rows_ref[left], wide_ref[right], preferred_element_type=jnp.float32)

    def folded(a):
        return jnp.sum(a.reshape(ROWS // 8, 8, ROWS), axis=0)

    def totals(exps, raw):
        teacher, student = exps[:, :ROWS], exps[:, ROWS:]
        gap = teacher * (raw[:, :ROWS] - raw[:, ROWS:])
        return folded(teacher), folded(student), folded(gap)

    def added(row, parts):
        for k, part in enumerate(parts):
            acc_ref[row, k] += part

    acc_ref[...] = jnp.zeros_like(acc_ref)

    def sum_turn(group, carry):
        done = []
        for k in range(UNROLL):
            word = plan_ref[LIST_AT + group * UNROLL + k]
            row, column = word >> 5, word & (BLOCKS - 1)
            raw = scores(column, row)
            done.append((row, totals(jnp.exp2(raw * (SCALE * LOG2E)), raw)))
        for row, parts in done:
            added(row, parts)
        return carry

    lax.fori_loop(0, (pairs + UNROLL - 1) // UNROLL, sum_turn, 0)

    def row_sums(k):
        return jnp.sum(acc_ref[:BLOCKS, k], axis=1)

    teacher_sum, student_sum, gap_sum = row_sums(0), row_sums(1), row_sums(2)
    fine = (
        (teacher_sum < SUM_LIMIT) & (student_sum < SUM_LIMIT) & (jnp.abs(gap_sum) < SUM_LIMIT)
    )
    safe = jnp.min(fine.astype(jnp.float32)) > 0.5
    grad_ref[...] = jnp.zeros_like(grad_ref)

    def finished(mean_div):
        high = mean_div.astype(jnp.bfloat16).astype(jnp.float32)
        middle = (mean_div - high).astype(jnp.bfloat16).astype(jnp.float32)
        low = mean_div - high - middle
        lane = lax.broadcasted_iota(jnp.int32, (ROWS, ROWS), 1)
        tail = jnp.where(lane == HEAD, high, jnp.where(lane == HEAD + 1, middle, low))
        for b, out_ref in enumerate(out_refs):
            moved = pltpu.roll(grad_ref[b] * WEIGHT, HEAD, 1)
            out_ref[...] = jnp.where(lane < HEAD, moved, tail).astype(jnp.bfloat16)

    def along_rows(row):
        return jnp.broadcast_to(row, (ROWS, ROWS)).T

    def mean_of(per_row):
        return jnp.sum(per_row, keepdims=True).reshape(1, 1) * (1.0 / (BLOCKS * ROWS))

    def gradient(word, weigh):
        b, column = word >> 5, word & (BLOCKS - 1)
        raw = scores(me ^ ((b & 3) << 3), column)
        symmetric = weigh(b, column, raw)
        return b, jnp.dot(
            symmetric.astype(jnp.bfloat16), rows_ref[column], preferred_element_type=jnp.float32
        )

    @pl.when(safe)
    def _():
        inv_ref[0] = 1.0 / teacher_sum
        inv_ref[1] = 1.0 / student_sum
        for b in range(LINE):
            for k in range(2):
                col_ref[b, k] = along_rows(inv_ref[k, pl.ds(me ^ (b << 3), 1), :])

        def weigh(b, column, raw):
            exps = jnp.exp2(raw * (SCALE * LOG2E))
            teacher_inv = col_ref[b, 0] + inv_ref[0, pl.ds(column, 1), :]
            student_inv = col_ref[b, 1] + inv_ref[1, pl.ds(column, 1), :]
            return exps[:, ROWS:] * student_inv - exps[:, :ROWS] * teacher_inv

        def grad_turn(group, carry):
            done = [
                gradient(plan_ref[OWN_AT + group * UNROLL + k], weigh) for k in range(UNROLL)
            ]
            for b, part in done:
                grad_ref[b] += part
            return carry

        lax.fori_loop(0, (own_pairs + UNROLL - 1) // UNROLL, grad_turn, 0)
        per_row = (
            gap_sum * inv_ref[0] * SCALE - jnp.log(teacher_sum) + jnp.log(student_sum)
        )
        finished(mean_of(per_row))

    @pl.when(jnp.logical_not(safe))
    def _():
        top_ref[...] = jnp.full_like(top_ref, FLOOR)

        def top_turn(n, carry):
            word = plan_ref[LIST_AT + n]
            row, column = word >> 5, word & (BLOCKS - 1)
            raw = jnp.max(scores(column, row), axis=0, keepdims=True) * SCALE
            top_ref[0, pl.ds(row, 1), :] = jnp.maximum(top_ref[0, pl.ds(row, 1), :], raw[:, :ROWS])
            top_ref[1, pl.ds(row, 1), :] = jnp.maximum(top_ref[1, pl.ds(row, 1), :], raw[:, ROWS:])
            return carry

        lax.fori_loop(0, pairs, top_turn, 0)
        acc_ref[...] = jnp.zeros_like(acc_ref)

        def shifted_turn(n, carry):
            word = plan_ref[LIST_AT + n]
            row, column = word >> 5, word & (BLOCKS - 1)
            raw = scores(column, row)
            top = jnp.concatenate(
                [top_ref[0, pl.ds(row, 1), :], top_ref[1, pl.ds(row, 1), :]], axis=1
            )
            added(row, totals(jnp.exp(raw * SCALE - top), raw))
            return carry

        lax.fori_loop(0, pairs, shifted_turn, 0)
        teacher_sum, student_sum, gap_sum = row_sums(0), row_sums(1), row_sums(2)
        inv_ref[0] = top_ref[0] + jnp.log(teacher_sum)
        inv_ref[1] = top_ref[1] + jnp.log(student_sum)
        for b in range(LINE):
            for k in range(2):
                col_ref[b, k] = along_rows(inv_ref[k, pl.ds(me ^ (b << 3), 1), :])

        def weigh(b, column, raw):
            teacher, student = raw[:, :ROWS] * SCALE, raw[:, ROWS:] * SCALE
            rows_gap = jnp.exp(student - col_ref[b, 1]) - jnp.exp(teacher - col_ref[b, 0])
            cols_gap = jnp.exp(student - inv_ref[1, pl.ds(column, 1), :]) - jnp.exp(
                teacher - inv_ref[0, pl.ds(column, 1), :]
            )
            return rows_gap + cols_gap

        def grad_turn(n, carry):
            b, part = gradient(plan_ref[OWN_AT + n], weigh)
            grad_ref[b] += part
            return carry

        lax.fori_loop(0, own_pairs, grad_turn, 0)
        finished(mean_of(gap_sum / teacher_sum * SCALE - inv_ref[0] + inv_ref[1]))


def assemble_kernel(*refs):
    in_refs, (grad_ref, div_ref) = refs[:LINE], refs[LINE:]
    x = my_index() >> 3
    lane = lax.broadcasted_iota(jnp.int32, (16, ROWS), 1)
    holds_div = (lane >= HEAD) & (lane < HEAD + 3) & (
        lax.broadcasted_iota(jnp.int32, (16, ROWS), 0) == 0
    )
    for case in range(LINE):

        @pl.when(x == case)
        def _():
            for head in range(LINE):
                from_ref = in_refs[head ^ case]
                grad_ref[:, head * HEAD : head * HEAD + HEAD] = from_ref[:, :HEAD]
                parts = jnp.where(holds_div, from_ref[:16].astype(jnp.float32), 0.0)
                div_ref[head] = jnp.sum(parts)


def per_device(teacher_q, student_q, owner_table):
    tile = jax.ShapeDtypeStruct((ROWS, ROWS), jnp.bfloat16)
    slices = pl.pallas_call(
        slice_kernel,
        out_shape=[tile] * LINE,
        in_specs=[VMEM, VMEM],
        out_specs=[VMEM] * LINE,
        name="slice_heads",
    )(teacher_q, student_q)
    plan = pl.pallas_call(
        plan_kernel,
        out_shape=jax.ShapeDtypeStruct((PLAN_LEN,), jnp.int32),
        in_specs=[SMEM],
        out_specs=SMEM,
        name="list_pairs",
    )(owner_table)
    line = jnp.stack([slices[0]] + [exchanged(slices[b], b << 3) for b in (1, 2, 3)])
    half = jnp.concatenate([line] + [exchanged(line, a << 1) for a in (1, 2, 3)])
    other = exchanged(half, 1)
    grads = pl.pallas_call(
        main_kernel,
        out_shape=[tile] * LINE,
        in_specs=[SMEM, VMEM, VMEM],
        out_specs=[VMEM] * LINE,
        scratch_shapes=[
            pltpu.VMEM((BLOCKS, ROWS, ROWS), jnp.bfloat16),
            pltpu.VMEM((BLOCKS + 1, ROWS, 2 * ROWS), jnp.bfloat16),
            pltpu.VMEM((BLOCKS + 1, 3, 8, ROWS), jnp.float32),
            pltpu.VMEM((2, BLOCKS, ROWS), jnp.float32),
            pltpu.VMEM((2, BLOCKS, ROWS), jnp.float32),
            pltpu.VMEM((LINE + 1, ROWS, ROWS), jnp.float32),
            pltpu.VMEM((LINE + 1, 2, ROWS, ROWS), jnp.float32),
        ],
        compiler_params=pltpu.CompilerParams(vmem_limit_bytes=24 << 20),
        name="sums_and_gradient",
    )(plan, half, other)
    back = [grads[0]] + [exchanged(grads[b], b << 3) for b in (1, 2, 3)]
    return pl.pallas_call(
        assemble_kernel,
        out_shape=[
            jax.ShapeDtypeStruct(teacher_q.shape, jnp.bfloat16),
            jax.ShapeDtypeStruct((LINE,), jnp.float32),
        ],
        in_specs=[VMEM] * LINE,
        out_specs=[VMEM, SMEM],
        name="assemble",
    )(*back)


def solution(mesh):
    placed = (P("tok", "head"), P("tok", "head"), P())
    return jax.shard_map(
        lambda *arrays: tuple(per_device(*arrays)),
        mesh=mesh,
        in_specs=placed,
        out_specs=(P("tok", "head"), P("head")),
        check_vma=False,
    )
```

time: 183 us -> 165 us (0.902); the launches traced: 180 us -> 168 us
  Pallas kernels: 0 us -> 138 us
  waiting for transfers between devices: 68 us -> 12.3 us
  starting transfers between devices: 38.8 us -> 14.3 us
  local copies, waits for them, and re-layouts: 26.6 us -> 2.81 us
  loops' own time: 18 us -> 0 us
  between operations: 14.1 us -> 0.71 us
  matrix products: 8.65 us -> 0 us
  other arithmetic: 6.1 us -> 0.02 us
    pallas_call x0 -> x4, Pallas kernels: none -> 138 us  [the longest x1 130 us: per_device(): pl.pallas_call(main_kernel, out_shape=[tile] * LINE, in_specs=[SMEM, VMEM...]
    all_gather x1 -> x0, waiting for transfers between devices: 53.6 us -> none  [sent_together(): whole, at, done = (lax.all_gather(both, axis, axis=dim, tiled=True), 0, [])]
    all_to_all x2 -> x0, starting transfers between devices: 38.8 us -> none  [copy_for_each(): return lax.all_to_all(copies, axis, split_axis=0, concat_axis=0, tiled=True)]
    dynamic_slice x36 -> x0, local copies, waits for them, and re-layouts: 18.5 us -> none  [the longest x18 10.5 us: gathered_block(): lax.dynamic_slice_in_dim(gathered, position * block_rows, block_rows, 0)]
    another operation x2 -> x0, loops' own time: 18 us -> none  [the longest x1 9.02 us: per_device(): lax.fori_loop(0, column_total, gradient_turn, (start_grad, jnp.zeros((hea...]
    all_to_all x2 -> x0, waiting for transfers between devices: 14.5 us -> none  [copy_for_each(): return lax.all_to_all(copies, axis, split_axis=0, concat_axis=0, tiled=True)]
    ppermute x0 -> x10, starting transfers between devices: none -> 14.3 us  [exchanged(): return lax.ppermute(array, 'tok', [(i, i ^ bits) for i in range(BLOCKS)])]
    ppermute x0 -> x10, waiting for transfers between devices: none -> 12.3 us  [exchanged(): return lax.ppermute(array, 'tok', [(i, i ^ bits) for i in range(BLOCKS)])]
  transfers between devices with their start and end apart: 3 -> 10, of which waited for: 3 -> 7; matrix products, arithmetic and copies ran while one was open for 3% -> 1% of each run, Pallas kernels for 0% -> 3%
where the time goes in v1:
time: 165 us; the launch traced here: 168 us
  Pallas kernels  138 us (84%)
  starting transfers between devices  14.3 us (9%)
  waiting for transfers between devices  12.3 us (7%)
  local copies, waits for them, and re-layouts  2.81 us (2%)
    pallas_call x1, Pallas kernels, per_device(): pl.pallas_call(main_kernel, out_shape=[tile] * LINE, in_specs=[SMEM, VMEM...  130 us
    ppermute x10, starting transfers between devices, exchanged(): return lax.ppermute(array, 'tok', [(i, i ^ bits) for i in range(BLOCKS)])  14.3 us
    ppermute x10, waiting for transfers between devices, exchanged(): return lax.ppermute(array, 'tok', [(i, i ^ bits) for i in range(BLOCKS)])  12.3 us
    pallas_call x1, Pallas kernels, per_device(): pl.pallas_call(plan_kernel, out_shape=jax.ShapeDtypeStruct((PLAN_LEN,), j...  4.42 us
  transfers between devices with their start and end apart: 10, of which 7 were waited for; matrix products, arithmetic and copies ran while one was open for 1% of the time, Pallas kernels for 3%

profile of v1, /device:TPU:32, one launch (start us, length us, event | category | flops | bytes accessed | tf_op | source)
XLA Modules:
  0.0 168.3 jit_solution(16135632971327156339)
XLA Ops:
  0.6 1.8 %slice_heads.1 = (bf16[128,128]{1,0:T(8,128)(2,1)}, bf16[128,128]{1,0:T(8,128)(2,1)}, bf16[128,128]{1,0:T(8,128)(2,1)}, bf16[128,128]{1,0:T(8,128)(2,1)}) custom-call(bf16[128,256]{1,0:T(8,128)(2,1)} %teacher_ref.1, bf16[128,256]{1,0:T(8,128)(2,1)} %student_ref.1), custom_call_target="tpu_custom_call" | custom-call | tf_op jit(solution)/shard_map/slice_heads/pallas_call | solution.py:253
  2.5 1.5 collective-permute-start
  4.0 2.7 %collective-permute-start.1 = (bf16[128,128]{1,0:T(8,128)(2,1)}, bf16[128,128]{1,0:T(8,128)(2,1)S(1)}, u32[]{:S(2)}, u32[]{:S(2)}) collective-permute-start(bf16[128,128]{1,0:T(8,128)(2,1)} %get-tuple-element.12), channel_id=1, source_target_pairs={{0,16},{1,17},{2,18},{3,19},{4,20},{5,21},{6,22},{7,23},{8,24},{9,... | collective-permute-start | bytes 98312 | tf_op jit(solution)/shard_map/ppermute | solution.py:31
  6.7 0.5 collective-permute-start.2
  7.2 0.0 copy-start.2
  7.2 0.8 constant_dynamic-update-slice_fusion.6
  8.0 0.0 collective-permute-done
  8.0 1.6 collective-permute-done.1
  9.6 2.4 %collective-permute-done.2 = bf16[128,128]{1,0:T(8,128)(2,1)S(1)} collective-permute-done((bf16[128,128]{1,0:T(8,128)(2,1)}, bf16[128,128]{1,0:T(8,128)(2,1)S(1)}, u32[]{:S(2)}, u32[]{:S(2)}) %collective-permute-start.2) | collective-permute-done | bytes 32800 | tf_op jit(solution)/shard_map/ppermute | solution.py:31
  12.0 0.0 copy-done.2
  12.0 1.7 collective-permute-start.3
  13.7 2.9 %collective-permute-start.4 = (bf16[4,128,128]{2,1,0:T(8,128)(2,1)S(1)}, bf16[4,128,128]{2,1,0:T(8,128)(2,1)S(1)}, u32[]{:S(2)}, u32[]{:S(2)}) collective-permute-start(bf16[4,128,128]{2,1,0:T(8,128)(2,1)S(1)} %pad_maximum_fusion), channel_id=1, source_target_pairs={{0,4},{1,5},{2,6},{3,7},{4,0},{5,1},{6,2},{7,3},{8,12},{9,13},{10,... | collective-permute-start | bytes 393224 | tf_op jit(solution)/shard_map/ppermute | solution.py:31
  16.6 0.2 collective-permute-start.5
  16.9 1.1 collective-permute-done.3
  18.0 3.0 %collective-permute-done.4 = bf16[4,128,128]{2,1,0:T(8,128)(2,1)S(1)} collective-permute-done((bf16[4,128,128]{2,1,0:T(8,128)(2,1)S(1)}, bf16[4,128,128]{2,1,0:T(8,128)(2,1)S(1)}, u32[]{:S(2)}, u32[]{:S(2)}) %collective-permute-start.4) | collective-permute-done | bytes 131104 | tf_op jit(solution)/shard_map/ppermute | solution.py:31
  21.0 1.8 %collective-permute-done.5 = bf16[4,128,128]{2,1,0:T(8,128)(2,1)S(1)} collective-permute-done((bf16[4,128,128]{2,1,0:T(8,128)(2,1)S(1)}, bf16[4,128,128]{2,1,0:T(8,128)(2,1)S(1)}, u32[]{:S(2)}, u32[]{:S(2)}) %collective-permute-start.5) | collective-permute-done | bytes 131104 | tf_op jit(solution)/shard_map/ppermute | solution.py:31
  22.8 0.1 collective-permute-start.6
  22.9 4.4 %list_pairs.1.plan_ref = s32[1176]{0:T(1024)} custom-call(s32[32,32]{1,0:T(8,128)} %table_ref.1), custom_call_target="tpu_custom_call" | custom-call | tf_op jit(solution)/shard_map/list_pairs/pallas_call | solution.py:260
  27.3 0.0 collective-permute-done.6.other_ref
  27.3 0.0 copy-start
  27.4 0.7 copy-done
  28.0 130.4 %sums_and_gradient.1 = (bf16[128,128]{1,0:T(8,128)(2,1)S(1)}, bf16[128,128]{1,0:T(8,128)(2,1)S(1)}, bf16[128,128]{1,0:T(8,128)(2,1)S(1)}, bf16[128,128]{1,0:T(8,128)(2,1)S(1)}) custom-call(s32[1176]{0:T(1024)S(1)} %copy-done, bf16[16,128,128]{2,1,0:T(8,128)(2,1)S(1)} %constant_dynamic-update-slice_fusion.half_ref, ...), custom_call_target="tpu_custom_call" | custom-call | tf_op jit(solution)/shard_map/sums_and_gradient/pallas_call | solution.py:270
  158.4 0.0 copy-start.1
  158.4 0.6 copy-done.1
  159.0 0.0 collective-permute-start.7
  159.0 1.9 %collective-permute-start.8 = (bf16[128,128]{1,0:T(8,128)(2,1)S(1)}, bf16[128,128]{1,0:T(8,128)(2,1)S(1)}, u32[]{:S(2)}, u32[]{:S(2)}) collective-permute-start(bf16[128,128]{1,0:T(8,128)(2,1)S(1)} %get-tuple-element.16), channel_id=1, source_target_pairs={{0,16},{1,17},{2,18},{3,19},{4,20},{5,21},{6,22},{7,23},{8,24},{9,... | collective-permute-start | bytes 98312 | tf_op jit(solution)/shard_map/ppermute | solution.py:31
  161.0 2.8 %collective-permute-start.9 = (bf16[128,128]{1,0:T(8,128)(2,1)S(1)}, bf16[128,128]{1,0:T(8,128)(2,1)S(1)}, u32[]{:S(2)}, u32[]{:S(2)}) collective-permute-start(bf16[128,128]{1,0:T(8,128)(2,1)S(1)} %get-tuple-element.17), channel_id=1, source_target_pairs={{0,24},{1,25},{2,26},{3,27},{4,28},{5,29},{6,30},{7,31},{8,16},{9,... | collective-permute-start | bytes 98312 | tf_op jit(solution)/shard_map/ppermute | solution.py:31
  163.7 0.0 collective-permute-done.7.refs_1_
  163.7 0.0 copy-start.3
  163.7 0.7 collective-permute-done.8.refs_2_
  164.4 0.0 copy-start.4
  164.4 1.6 collective-permute-done.9.refs_3_
  166.1 0.0 copy-start.5
  166.1 0.0 copy-done.3
  166.1 0.0 copy-done.4
  166.1 0.6 copy-done.5
  166.7 1.6 assemble.1
  (7 shorter events, 0.1 us)
Async XLA Ops:
  2.5 5.5 %collective-permute-start = (bf16[128,128]{1,0:T(8,128)(2,1)}, bf16[128,128]{1,0:T(8,128)(2,1)S(1)}, u32[]{:S(2)}, u32[]{:S(2)}) collective-permute-start(bf16[128,128]{1,0:T(8,128)(2,1)} %get-tuple-element.11), channel_id=1, source_target_pairs={{0,8},{1,9},{2,10},{3,11},{4,12},{5,13},{6,14},{7,15},{8,0},{9,1},... | collective-permute-start | bytes 98312 | tf_op jit(solution)/shard_map/ppermute | solution.py:31
  4.0 5.6 %collective-permute-start.1 = (bf16[128,128]{1,0:T(8,128)(2,1)}, bf16[128,128]{1,0:T(8,128)(2,1)S(1)}, u32[]{:S(2)}, u32[]{:S(2)}) collective-permute-start(bf16[128,128]{1,0:T(8,128)(2,1)} %get-tuple-element.12), channel_id=1, source_target_pairs={{0,16},{1,17},{2,18},{3,19},{4,20},{5,21},{6,22},{7,23},{8,24},{9,... | collective-permute-start | bytes 98312 | tf_op jit(solution)/shard_map/ppermute | solution.py:31
  6.7 5.3 %collective-permute-start.2 = (bf16[128,128]{1,0:T(8,128)(2,1)}, bf16[128,128]{1,0:T(8,128)(2,1)S(1)}, u32[]{:S(2)}, u32[]{:S(2)}) collective-permute-start(bf16[128,128]{1,0:T(8,128)(2,1)} %get-tuple-element.13), channel_id=1, source_target_pairs={{0,24},{1,25},{2,26},{3,27},{4,28},{5,29},{6,30},{7,31},{8,16},{9,... | collective-permute-start | bytes 98312 | tf_op jit(solution)/shard_map/ppermute | solution.py:31
  7.2 4.9 %copy-start.2 = (bf16[128,128]{1,0:T(8,128)(2,1)S(1)}, bf16[128,128]{1,0:T(8,128)(2,1)}, u32[]{:S(2)}) copy-start(bf16[128,128]{1,0:T(8,128)(2,1)} %get-tuple-element.10) | copy-start | bytes 98308
  12.0 5.9 %collective-permute-start.3 = (bf16[4,128,128]{2,1,0:T(8,128)(2,1)S(1)}, bf16[4,128,128]{2,1,0:T(8,128)(2,1)S(1)}, u32[]{:S(2)}, u32[]{:S(2)}) collective-permute-start(bf16[4,128,128]{2,1,0:T(8,128)(2,1)S(1)} %pad_maximum_fusion), channel_id=1, source_target_pairs={{0,2},{1,3},{2,0},{3,1},{4,6},{5,7},{6,4},{7,5},{8,10},{9,11},{10,... | collective-permute-start | bytes 393224 | tf_op jit(solution)/shard_map/ppermute | solution.py:31
  13.7 7.2 %collective-permute-start.4 = (bf16[4,128,128]{2,1,0:T(8,128)(2,1)S(1)}, bf16[4,128,128]{2,1,0:T(8,128)(2,1)S(1)}, u32[]{:S(2)}, u32[]{:S(2)}) collective-permute-start(bf16[4,128,128]{2,1,0:T(8,128)(2,1)S(1)} %pad_maximum_fusion), channel_id=1, source_target_pairs={{0,4},{1,5},{2,6},{3,7},{4,0},{5,1},{6,2},{7,3},{8,12},{9,13},{10,... | collective-permute-start | bytes 393224 | tf_op jit(solution)/shard_map/ppermute | solution.py:31
  16.6 6.2 %collective-permute-start.5 = (bf16[4,128,128]{2,1,0:T(8,128)(2,1)S(1)}, bf16[4,128,128]{2,1,0:T(8,128)(2,1)S(1)}, u32[]{:S(2)}, u32[]{:S(2)}) collective-permute-start(bf16[4,128,128]{2,1,0:T(8,128)(2,1)S(1)} %pad_maximum_fusion), channel_id=1, source_target_pairs={{0,6},{1,7},{2,4},{3,5},{4,2},{5,3},{6,0},{7,1},{8,14},{9,15},{10,... | collective-permute-start | bytes 393224 | tf_op jit(solution)/shard_map/ppermute | solution.py:31
  22.8 4.5 %collective-permute-start.6 = (bf16[16,128,128]{2,1,0:T(8,128)(2,1)S(1)}, bf16[16,128,128]{2,1,0:T(8,128)(2,1)S(1)}, u32[]{:S(2)}, u32[]{:S(2)}) collective-permute-start(bf16[16,128,128]{2,1,0:T(8,128)(2,1)S(1)} %constant_dynamic-update-slice_fusion.half_ref), channel_id=1, source_target_pairs={{0,1},{1,0},{2,3},{3,2},{4,5},{5,4},{6,7},{7,6},{8,9},{9,8},{10,11... | collective-permute-start | bytes 1572872 | tf_op jit(solution)/shard_map/ppermute | solution.py:31
  27.3 0.7 copy-start
  158.4 0.6 copy-start.1
  159.0 4.7 %collective-permute-start.7 = (bf16[128,128]{1,0:T(8,128)(2,1)S(1)}, bf16[128,128]{1,0:T(8,128)(2,1)S(1)}, u32[]{:S(2)}, u32[]{:S(2)}) collective-permute-start(bf16[128,128]{1,0:T(8,128)(2,1)S(1)} %get-tuple-element.15), channel_id=1, source_target_pairs={{0,8},{1,9},{2,10},{3,11},{4,12},{5,13},{6,14},{7,15},{8,0},{9,1},... | collective-permute-start | bytes 98312 | tf_op jit(solution)/shard_map/ppermute | solution.py:31
  159.0 5.4 %collective-permute-start.8 = (bf16[128,128]{1,0:T(8,128)(2,1)S(1)}, bf16[128,128]{1,0:T(8,128)(2,1)S(1)}, u32[]{:S(2)}, u32[]{:S(2)}) collective-permute-start(bf16[128,128]{1,0:T(8,128)(2,1)S(1)} %get-tuple-element.16), channel_id=1, source_target_pairs={{0,16},{1,17},{2,18},{3,19},{4,20},{5,21},{6,22},{7,23},{8,24},{9,... | collective-permute-start | bytes 98312 | tf_op jit(solution)/shard_map/ppermute | solution.py:31
  161.0 5.1 %collective-permute-start.9 = (bf16[128,128]{1,0:T(8,128)(2,1)S(1)}, bf16[128,128]{1,0:T(8,128)(2,1)S(1)}, u32[]{:S(2)}, u32[]{:S(2)}) collective-permute-start(bf16[128,128]{1,0:T(8,128)(2,1)S(1)} %get-tuple-element.17), channel_id=1, source_target_pairs={{0,24},{1,25},{2,26},{3,27},{4,28},{5,29},{6,30},{7,31},{8,16},{9,... | collective-permute-start | bytes 98312 | tf_op jit(solution)/shard_map/ppermute | solution.py:31
  163.7 2.4 %copy-start.3 = (bf16[128,128]{1,0:T(8,128)(2,1)}, bf16[128,128]{1,0:T(8,128)(2,1)S(1)}, u32[]{:S(2)}) copy-start(bf16[128,128]{1,0:T(8,128)(2,1)S(1)} %collective-permute-done.7.refs_1_) | copy-start | bytes 98308
  164.4 1.7 copy-start.4
  166.1 0.6 copy-start.5
